TPU v7x, 256 devices: a whole 4x4x8 slice. The times are simulated.
256 devices in a mesh: energy: 16 (over x_lo, z), slab: 16 (over y, x_hi, core).
Axes of the slice: x: 4 (x_hi: 2, x_lo: 2; x = x_hi * 2 + x_lo), y: 4, z: 8, core: 2. Of those that a mesh axis runs over, the one named last changes fastest.
Arguments:
- onsite: float32 [16, 256], P('slab'), may hold values from -1 to 1
- hopping: float32 [16, 256, 256], P('slab'), may hold values from -0.12 to 0.12
- coupling: float32 [16, 256], P('slab'), may hold values from 0.4 to 0.8
- boundary_green: float32 [2, 16, 32, 256, 256], P(None, 'slab', 'energy'), may hold values from -0.09 to 0.09
- damping: float32 [16, 32], P('slab', 'energy'), may hold values from 1.5 to 6
- occupation: float32 [16, 32], P('slab', 'energy'), may hold values from 0 to 1
- tile_map: int32 [16, 128, 128], P('slab'), may hold values from 0 to 255
- prev_potential: float32 [16, 128, 128], P('slab'), may hold values from -6 to 6
Outputs:
- lesser_diag: float32 [16, 32, 256], P('slab', 'energy')
- potential: float32 [16, 128, 128], P('slab', 'energy')
All inputs are finite; a program needn't handle non-finite values.
Results may differ from a plain program's by a relative error of at most 0.0003.
Values sent between devices are 32-bit elements; how exact they have to be, the bound alone decides.
A program may use at most 64 MiB of HBM per device.

v0:
```python
import functools

import jax
import jax.numpy as jnp
import numpy as np
from jax import lax
from jax.experimental import pallas as pl
from jax.experimental.pallas import tpu as pltpu
from jax.sharding import PartitionSpec as P

F32 = jnp.float32
BF16 = jnp.bfloat16
MESH = pl.DeviceIdType.MESH
PHONON = 0.5
CHARGE = 2.0
ANISO = 0.05
SCREEN = 0.05
ROWS = 64


def line_tables(count):
    main = 2.0 + 4.0 * ANISO + SCREEN
    matrix = main * np.eye(count) - np.eye(count, k=1) - np.eye(count, k=-1)
    inverse = np.linalg.inv(matrix)
    around = (np.arange(count)[:, None] + np.arange(count)[None, :]) % count
    rows = np.arange(count)[:, None]
    return np.stack([inverse[rows, around], (inverse @ inverse)[rows, around]]).astype(np.float32)


def halves(value):
    high = value.astype(BF16)
    return high, (value - high.astype(F32)).astype(BF16)


def split(real, imag):
    return halves(real), halves(imag), halves(real + imag)


def times(first, second, turned):
    contract = (((1,), (1,)), ((), ())) if turned else (((1,), (0,)), ((), ()))

    def dot(a, b):
        return lax.dot_general(a, b, contract, preferred_element_type=F32)

    return dot(first[0], second[0]) + dot(first[0], second[1]) + dot(first[1], second[0])


def product(left, right, turned=False):
    one = times(left[0], right[0], turned)
    two = times(left[1], right[1], turned)
    both = times(left[2], right[2], turned)
    return one - two, both - one - two


def born_kernel(
    axis_sizes,
    green,
    hopping,
    onsite,
    coupling,
    damping,
    occupation,
    out,
    from_left,
    from_right,
    self_energy,
    facts,
    columns,
    block,
    phonon,
    slab_send,
    slab_recv,
    energy_send,
    energy_recv,
    fact_send,
    fact_recv,
):
    energies, slabs = axis_sizes
    e, s = lax.axis_index("energy"), lax.axis_index("slab")
    here = hopping.shape[-1]
    chunks = here // ROWS
    owned = 2
    has = {
        "left": s > 0,
        "right": s < slabs - 1,
        "below": e > 0,
        "above": e < energies - 1,
    }
    device = {"left": (e, s - 1), "right": (e, s + 1), "below": (e - 1, s), "above": (e + 1, s)}

    facts[3, 0:1, :] = coupling[...]
    for k in range(owned):
        facts[3, 1 + k : 2 + k, :] = jnp.full((1, here), damping[0, k], F32)
        facts[3, 3 + k : 4 + k, :] = jnp.full((1, here), occupation[0, k], F32)

    barrier = pltpu.get_barrier_semaphore()
    for side in ("left", "right", "below", "above"):

        @pl.when(has[side])
        def _():
            pl.semaphore_signal(barrier, inc=1, device_id=device[side], device_id_type=MESH)

    pl.semaphore_wait(barrier, sum(has[side].astype(jnp.int32) for side in has))

    def slab_copy(side, c):
        k, row = c // chunks, pl.multiple_of(lax.rem(c, chunks) * ROWS, ROWS)
        index = 0 if side == "right" else 1
        landing = from_left if side == "right" else from_right
        return pltpu.make_async_remote_copy(
            src_ref=green.at[:, 0, k, pl.ds(row, ROWS), :],
            dst_ref=landing.at[c],
            send_sem=slab_send.at[index, c],
            recv_sem=slab_recv.at[index, c],
            device_id=device[side],
            device_id_type=MESH,
        )

    def energy_copy(side, c):
        k, row = c // chunks, pl.multiple_of(lax.rem(c, chunks) * ROWS, ROWS)
        index = 0 if side == "above" else 1
        return pltpu.make_async_remote_copy(
            src_ref=self_energy.at[0, k, :, pl.ds(row, ROWS), :],
            dst_ref=self_energy.at[1 + index, k, :, pl.ds(row, ROWS), :],
            send_sem=energy_send.at[index, c],
            recv_sem=energy_recv.at[index, c],
            device_id=device[side],
            device_id_type=MESH,
        )

    def fact_copy(side):
        index = {"right": 0, "above": 1, "below": 2}[side]
        return pltpu.make_async_remote_copy(
            src_ref=facts.at[3],
            dst_ref=facts.at[index],
            send_sem=fact_send.at[index],
            recv_sem=fact_recv.at[index],
            device_id=device[side],
            device_id_type=MESH,
        )

    @pl.when(has["right"])
    def _():
        fact_copy("right").start()

    def send_green(c, carry):
        @pl.when(has["right"])
        def _():
            slab_copy("right", c).start()

        @pl.when(has["left"])
        def _():
            slab_copy("left", c).start()

        return carry

    lax.fori_loop(0, owned * chunks, send_green, 0)

    for side in ("above", "below"):

        @pl.when(has[side])
        def _():
            fact_copy(side).start()

    rows = lax.broadcasted_iota(jnp.int32, (here, here), 0)
    lanes = lax.broadcasted_iota(jnp.int32, (here, here), 1)

    def column(row):
        return jnp.sum(jnp.where(rows == lanes, row, 0.0), axis=1, keepdims=True)

    columns[:, 0:1] = column(onsite[...])
    columns[:, 1:2] = column(coupling[...])

    @pl.when(jnp.logical_not(has["left"]))
    def _():
        from_left[...] = jnp.zeros_like(from_left)
        facts[0] = jnp.zeros_like(facts[0])

    @pl.when(jnp.logical_not(has["right"]))
    def _():
        from_right[...] = jnp.zeros_like(from_right)

    @pl.when(has["left"])
    def _():
        fact_copy("right").wait_recv()

    columns[:, 2:3] = column(facts[0, 0:1, :])

    def form_self_energy(c, carry):
        k, row = c // chunks, pl.multiple_of(lax.rem(c, chunks) * ROWS, ROWS)

        @pl.when(has["left"])
        def _():
            slab_copy("right", c).wait_recv()

        @pl.when(has["right"])
        def _():
            slab_copy("left", c).wait_recv()

        weight_left = columns[pl.ds(row, ROWS), 2:3] * facts[0, 0:1, :]
        weight_right = columns[pl.ds(row, ROWS), 1:2] * facts[3, 0:1, :]
        for part in range(2):
            self_energy[0, k, part, pl.ds(row, ROWS), :] = (
                weight_left * from_left[c, part] + weight_right * from_right[c, part]
            )
        for side in ("above", "below"):

            @pl.when(has[side])
            def _():
                energy_copy(side, c).start()

        return carry

    def diagonal_inverse(energy, level, damp):
        real = energy - level
        modulus = real * real + damp * damp
        return real / modulus, -damp / modulus

    def step(t, carry):
        k, kind = t // 3, lax.rem(t, 3)
        lax.fori_loop(
            jnp.where(t == 0, 0, jnp.minimum(owned * chunks - 3 + t, owned * chunks)),
            jnp.minimum(owned * chunks - 2 + t, owned * chunks),
            form_self_energy,
            0,
        )
        slot = jnp.where(kind == 2, 0, 1 + kind)
        fact = jnp.where(kind == 2, 3, 1 + kind)
        present = jnp.where(kind == 0, e, jnp.where(kind == 1, energies - 1 - e, 1)) > 0

        def arrive(side):
            def one(c, inner):
                energy_copy(side, c).wait_recv()
                return inner

            lax.fori_loop(k * chunks, (k + 1) * chunks, one, 0)

            @pl.when(k == 0)
            def _():
                fact_copy(side).wait_recv()

        @pl.when((kind == 0) & has["below"])
        def _():
            arrive("above")

        @pl.when((kind == 1) & has["above"])
        def _():
            arrive("below")

        @pl.when(kind == 0)
        def _():
            phonon[...] = jnp.zeros_like(phonon)

        @pl.when(present)
        def _():
            place = owned * (e + jnp.where(kind == 2, 0, 2 * kind - 1)) + k
            energy = -2.0 + 4.0 * (place.astype(F32) + 0.5) / (owned * energies)
            damp = facts[fact, pl.ds(1 + k, 1), :]
            x_real, x_imag = diagonal_inverse(energy, onsite[...], damp)
            se_real, se_imag = self_energy[slot, k, 0], self_energy[slot, k, 1]

            @pl.when(kind < 2)
            def _():
                block[0] = hopping[0] + se_real
                block[1] = se_imag

            @pl.when(kind == 2)
            def _():
                block[0] = hopping[0] + se_real + phonon[0]
                block[1] = se_imag + phonon[1]

            h_real, h_imag = block[0], block[1]
            a_real = h_real * x_real - h_imag * x_imag
            a_imag = h_real * x_imag + h_imag * x_real
            a = split(a_real, a_imag)
            square = product(a, a)
            two = split(*square)
            cube = product(a, two)
            fourth = product(two, two)
            t_real = a_real + square[0] + cube[0]
            t_imag = a_imag + square[1] + cube[1]
            rest = product(split(t_real, t_imag), split(*fourth))
            t_real = t_real + fourth[0] + rest[0]
            t_imag = t_imag + fourth[1] + rest[1]
            series = split(t_real, t_imag)

            fill = facts[fact, pl.ds(3 + k, 1), :]
            sigma_real = -fill * (se_real - se_real.T)
            sigma_imag = -fill * (se_imag + se_imag.T)

            @pl.when(kind < 2)
            def _():
                more = product(series, split(sigma_real, sigma_imag))
                w_real, w_imag = sigma_real + more[0], sigma_imag + more[1]
                adjoint = (series[0], halves(-t_imag), halves(t_real - t_imag))
                more = product(split(w_real, w_imag), adjoint, True)
                u_real, u_imag = w_real + more[0], w_imag + more[1]
                c_real, c_imag = diagonal_inverse(energy, columns[:, 0:1], damp[:, 0:1])
                c_real, c_imag = PHONON * c_real, PHONON * c_imag
                v_real = c_real * u_real - c_imag * u_imag
                v_imag = c_real * u_imag + c_imag * u_real
                unit = jnp.where(rows == lanes, 1.0, 0.0)
                g_real = unit + t_real
                phonon[0] += c_real * g_real - c_imag * t_imag
                phonon[1] += c_real * t_imag + c_imag * g_real
                phonon[2] += v_real * x_real + v_imag * x_imag
                phonon[3] += v_imag * x_real - v_real * x_imag

            @pl.when(kind == 2)
            def _():
                mixed_real = sigma_real + phonon[2]
                mixed_imag = sigma_imag + phonon[3]
                more = product(series, split(mixed_real, mixed_imag))
                w_real, w_imag = mixed_real + more[0], mixed_imag + more[1]
                terms = w_imag * t_real - w_real * t_imag + jnp.where(rows == lanes, w_imag, 0.0)
                total = jnp.sum(terms.T, axis=0, keepdims=True)
                out[pl.ds(k, 1), :] = (x_real * x_real + x_imag * x_imag) * total

        return carry

    lax.fori_loop(0, 3 * owned, step, 0)

    def settle(c, carry):
        for side in ("right", "left"):

            @pl.when(has[side])
            def _():
                slab_copy(side, c).wait_send()

        for side in ("above", "below"):

            @pl.when(has[side])
            def _():
                energy_copy(side, c).wait_send()

        return carry

    lax.fori_loop(0, owned * chunks, settle, 0)
    for side in ("right", "above", "below"):

        @pl.when(has[side])
        def _():
            fact_copy(side).wait_send()


def born(axis_sizes, green, hopping, onsite, coupling, damping, occupation):
    size = hopping.shape[-1]
    count = 2 * (size // ROWS)
    vmem, smem = pl.BlockSpec(memory_space=pltpu.VMEM), pl.BlockSpec(memory_space=pltpu.SMEM)
    return pl.pallas_call(
        functools.partial(born_kernel, axis_sizes),
        out_shape=jax.ShapeDtypeStruct((2, size), F32),
        in_specs=[pl.BlockSpec(memory_space=pl.ANY), vmem, vmem, vmem, smem, smem],
        out_specs=vmem,
        scratch_shapes=[
            pltpu.VMEM((count, 2, ROWS, size), F32),
            pltpu.VMEM((count, 2, ROWS, size), F32),
            pltpu.VMEM((3, 2, 2, size, size), F32),
            pltpu.VMEM((4, 8, size), F32),
            pltpu.VMEM((size, 128), F32),
            pltpu.VMEM((2, size, size), F32),
            pltpu.VMEM((4, size, size), F32),
            pltpu.SemaphoreType.DMA((2, count)),
            pltpu.SemaphoreType.DMA((2, count)),
            pltpu.SemaphoreType.DMA((2, count)),
            pltpu.SemaphoreType.DMA((2, count)),
            pltpu.SemaphoreType.DMA((3,)),
            pltpu.SemaphoreType.DMA((3,)),
        ],
        compiler_params=pltpu.CompilerParams(
            collective_id=0, has_side_effects=True, vmem_limit_bytes=50 << 20
        ),
        name="born",
    )(green, hopping, onsite, coupling, damping, occupation)


def poisson_kernel(
    axis_sizes,
    lesser,
    tile_map,
    previous,
    tables,
    out,
    densities,
    weighted,
    landed,
    density_send,
    density_recv,
    plane_send,
    plane_recv,
):
    energies, slabs = axis_sizes
    e, s = lax.axis_index("energy"), lax.axis_index("slab")
    rows = out.shape[1]
    width = out.shape[2]
    barrier = pltpu.get_barrier_semaphore()
    for d in range(1, energies):
        pl.semaphore_signal(
            barrier, inc=1, device_id=(lax.rem(e + d, energies), s), device_id_type=MESH
        )
    for d in range(1, slabs):
        pl.semaphore_signal(
            barrier, inc=1, device_id=(e, lax.rem(s + d, slabs)), device_id_type=MESH
        )
    densities[e] = (4.0 / (2 * energies)) * jnp.sum(lesser[...], axis=0, keepdims=True)
    pl.semaphore_wait(barrier, energies + slabs - 2)

    def density_copy(d):
        return pltpu.make_async_remote_copy(
            src_ref=densities.at[e],
            dst_ref=densities.at[e],
            send_sem=density_send.at[d],
            recv_sem=density_recv.at[d],
            device_id=(lax.rem(e + d, energies), s),
            device_id_type=MESH,
        )

    def density_landing(d):
        slot = lax.rem(e + energies - d, energies)
        return pltpu.make_async_remote_copy(
            src_ref=densities.at[slot],
            dst_ref=densities.at[slot],
            send_sem=density_send.at[d],
            recv_sem=density_recv.at[d],
            device_id=(lax.rem(e + d, energies), s),
            device_id_type=MESH,
        )

    def plane_copy(d):
        return pltpu.make_async_remote_copy(
            src_ref=weighted.at[d],
            dst_ref=landed.at[d],
            send_sem=plane_send.at[d],
            recv_sem=plane_recv.at[d],
            device_id=(e, lax.rem(s + d, slabs)),
            device_id_type=MESH,
        )

    for d in range(1, energies):
        density_copy(d).start()

    def blocks(ref):
        own = ref[0, pl.ds(pl.multiple_of(e * rows, rows), rows), :]
        before = ref[0, pl.ds(pl.multiple_of(jnp.maximum(e - 1, 0) * rows, rows), rows), :]
        after = ref[
            0, pl.ds(pl.multiple_of(jnp.minimum(e + 1, energies - 1) * rows, rows), rows), :
        ]
        return before, own, after

    lane = lax.broadcasted_iota(jnp.int32, (3 * rows, width), 1)
    line = lax.broadcasted_iota(jnp.int32, (3 * rows, width), 0) + (e - 1) * rows
    inside = (line >= 0) & (line < energies * rows)

    def beside(field):
        up = pltpu.roll(field, 1, 0)
        down = pltpu.roll(field, 3 * rows - 1, 0)
        left = jnp.where(lane == 0, 0.0, pltpu.roll(field, 1, 1))
        right = jnp.where(lane == width - 1, 0.0, pltpu.roll(field, width - 1, 1))
        return up + down + left + right

    potential = jnp.where(inside, jnp.concatenate(blocks(previous), axis=0), 0.0)
    potential = jnp.where(inside, beside(potential), 0.0)
    potential = (ANISO * ANISO) * beside(potential)[rows : 2 * rows]
    index = jnp.concatenate(blocks(tile_map), axis=0)

    for d in range(1, energies):
        density_landing(d).wait_recv()
    density = CHARGE * jnp.sum(densities[...], axis=0)

    def spread(half):
        table = jnp.broadcast_to(density[:, half * width : (half + 1) * width], (3 * rows, width))
        return jnp.take_along_axis(table, index & (width - 1), axis=1)

    source = jnp.where(inside, jnp.where(index < width, spread(0), spread(1)), 0.0)
    second = ANISO * beside(source)[rows : 2 * rows] + potential
    source = source[rows : 2 * rows]
    for d in range(1, slabs):
        weighted[d] = tables[0, s, d] * source + tables[1, s, d] * second
        plane_copy(d).start()
    total = tables[0, s, 0] * source + tables[1, s, 0] * second
    for d in range(1, slabs):
        plane_copy(d).wait_recv()
        total = total + landed[d]
    out[0] = total
    for d in range(1, energies):
        density_copy(d).wait_send()
    for d in range(1, slabs):
        plane_copy(d).wait_send()


def poisson(axis_sizes, lesser, tile_map, previous, tables):
    energies, slabs = axis_sizes
    rows, width = tile_map.shape[1] // energies, tile_map.shape[2]
    vmem, smem = pl.BlockSpec(memory_space=pltpu.VMEM), pl.BlockSpec(memory_space=pltpu.SMEM)
    return pl.pallas_call(
        functools.partial(poisson_kernel, axis_sizes),
        out_shape=jax.ShapeDtypeStruct((1, rows, width), F32),
        in_specs=[vmem, vmem, vmem, smem],
        out_specs=vmem,
        scratch_shapes=[
            pltpu.VMEM((energies, 1, lesser.shape[1]), F32),
            pltpu.VMEM((slabs, rows, width), F32),
            pltpu.VMEM((slabs, rows, width), F32),
            pltpu.SemaphoreType.DMA((energies,)),
            pltpu.SemaphoreType.DMA((energies,)),
            pltpu.SemaphoreType.DMA((slabs,)),
            pltpu.SemaphoreType.DMA((slabs,)),
        ],
        compiler_params=pltpu.CompilerParams(
            collective_id=1, has_side_effects=True, vmem_limit_bytes=16 << 20
        ),
        name="poisson",
    )(lesser, tile_map, previous, tables)


def solution(mesh):
    axis_sizes = (mesh.shape["energy"], mesh.shape["slab"])
    tables = line_tables(axis_sizes[1])

    def per_device(onsite, hopping, coupling, green, damping, occupation, tile_map, previous):
        lesser = born(axis_sizes, green, hopping, onsite, coupling, damping, occupation)
        potential = poisson(axis_sizes, lesser, tile_map, previous, jnp.asarray(tables))
        return lesser[None], potential

    in_specs = (
        P("slab", None),
        P("slab", None, None),
        P("slab", None),
        P(None, "slab", "energy", None, None),
        P("slab", "energy"),
        P("slab", "energy"),
        P("slab", None, None),
        P("slab", None, None),
    )
    out_specs = (P("slab", "energy", None), P("slab", "energy", None))
    return jax.shard_map(
        per_device, mesh=mesh, in_specs=in_specs, out_specs=out_specs, check_vma=False
    )
```

profile of v0, /device:TPU:1, one launch (start us, length us, event | category | flops | bytes accessed | tf_op | source)
XLA Modules:
  0.0 90.5 jit_solution(14810195402846853976)
XLA Ops:
  0.6 0.0 copy-start
  0.6 1.2 %copy-done = f32[2,1,2,256,256]{4,3,2,1,0:T(8,128)S(1)} copy-done((f32[2,1,2,256,256]{4,3,2,1,0:T(8,128)S(1)}, f32[2,1,2,256,256]{4,3,2,1,0:T(8,128)}, u32[]{:S(2)}) %copy-start) | copy-done | bytes 1048600
  1.9 0.0 copy-start.1
  1.9 0.9 %copy-done.1 = f32[1,256,256]{2,1,0:T(8,128)S(1)} copy-done((f32[1,256,256]{2,1,0:T(8,128)S(1)}, f32[1,256,256]{2,1,0:T(8,128)}, u32[]{:S(2)}) %copy-start.1) | copy-done | bytes 262168
  2.8 0.0 copy-start.5
  2.8 0.7 copy-done.5
  3.5 0.0 copy-start.6
  3.5 0.7 copy-done.6
  4.2 0.0 copy-start.7
  4.2 0.7 copy-done.7
  4.8 0.0 copy-start.8
  4.8 0.7 copy-done.8
  5.5 0.0 copy-start.2
  5.5 0.0 copy-start.3
  5.5 0.0 copy-start.4
  5.5 62.5 %born.1.lesser = f32[2,256]{1,0:T(2,128)S(1)} custom-call(f32[2,1,2,256,256]{4,3,2,1,0:T(8,128)S(1)} %copy-done, f32[1,256,256]{2,1,0:T(8,128)S(1)} %copy-done.1, f32[1,256]{1,0:T(1,128)S(1)} %copy-done.5, f32[1,256]{1,0:T(1,128)S(1)} %copy-done.6, f32[1,2]{1,0:T(1,128)S(1)} %copy-done.7, f32[1,2]{1,0:T(1,128)S(1)} %copy-done.8), custom_call_target="tpu_custom_call" | custom-call | tf_op jit(solution)/shard_map/born/pallas_call | solution.py:349
  68.0 0.0 copy-done.2
  68.0 0.0 copy-done.3
  68.0 0.0 copy-done.4
  68.0 21.3 %poisson.1 = f32[1,8,128]{2,1,0:T(8,128)S(1)} custom-call(f32[2,256]{1,0:T(2,128)S(1)} %born.1.lesser, s32[1,128,128]{2,1,0:T(8,128)S(1)} %copy-done.2, f32[1,128,128]{2,1,0:T(8,128)S(1)} %copy-done.3, f32[2,16,16]{2,1,0:T(8,128)S(1)} %copy-done.4), custom_call_target="tpu_custom_call" | custom-call | tf_op jit(solution)/shard_map/poisson/pallas_call | solution.py:494
  89.3 0.6 copy.13
  89.9 0.6 copy.14
Async XLA Ops:
  0.6 1.2 %copy-start = (f32[2,1,2,256,256]{4,3,2,1,0:T(8,128)S(1)}, f32[2,1,2,256,256]{4,3,2,1,0:T(8,128)}, u32[]{:S(2)}) copy-start(f32[2,1,2,256,256]{4,3,2,1,0:T(8,128)} %green.1) | copy-start | bytes 3145732
  1.9 0.9 %copy-start.1 = (f32[1,256,256]{2,1,0:T(8,128)S(1)}, f32[1,256,256]{2,1,0:T(8,128)}, u32[]{:S(2)}) copy-start(f32[1,256,256]{2,1,0:T(8,128)} %hopping.1) | copy-start | bytes 786436
  2.8 0.7 copy-start.5
  3.5 0.7 copy-start.6
  4.2 0.7 copy-start.7
  4.8 0.7 copy-start.8
  5.5 62.5 %copy-start.2 = (s32[1,128,128]{2,1,0:T(8,128)S(1)}, s32[1,128,128]{2,1,0:T(8,128)}, u32[]{:S(2)}) copy-start(s32[1,128,128]{2,1,0:T(8,128)} %tile_map.1) | copy-start | bytes 196612
  5.5 62.5 %copy-start.3 = (f32[1,128,128]{2,1,0:T(8,128)S(1)}, f32[1,128,128]{2,1,0:T(8,128)}, u32[]{:S(2)}) copy-start(f32[1,128,128]{2,1,0:T(8,128)} %previous.1) | copy-start | bytes 196612
  5.5 62.5 %copy-start.4 = (f32[2,16,16]{2,1,0:T(8,128)S(1)}, f32[2,16,16]{2,1,0:T(8,128)}, u32[]{:S(2)}) copy-start(f32[2,16,16]{2,1,0:T(8,128)} %constant.2.clone.tables) | copy-start | bytes 6148
where the time goes:
time: 90.7 us; the launch traced here: 90.5 us
  Pallas kernels  83.8 us (92%)
  local copies, waits for them, and re-layouts  6.02 us (7%)
    pallas_call x1, Pallas kernels, born(): pl.pallas_call(functools.partial(born_kernel, axis_sizes), out_shape=jax....  62.5 us
    pallas_call x1, Pallas kernels, poisson(): pl.pallas_call(functools.partial(poisson_kernel, axis_sizes), out_shape=j...  21.3 us
    unnamed x20, local copies, waits for them, and re-layouts  6.02 us

commit v1 on v0

--- a/solution.py
+++ b/solution.py
@@ -15,7 +15,7 @@
 CHARGE = 2.0
 ANISO = 0.05
 SCREEN = 0.05
-ROWS = 64
+ROWS = 32
 
 
 def line_tables(count):
@@ -24,7 +24,8 @@
     inverse = np.linalg.inv(matrix)
     around = (np.arange(count)[:, None] + np.arange(count)[None, :]) % count
     rows = np.arange(count)[:, None]
-    return np.stack([inverse[rows, around], (inverse @ inverse)[rows, around]]).astype(np.float32)
+    weights = np.stack([inverse[rows, around], (inverse @ inverse)[rows, around]], axis=-1)
+    return np.repeat(weights[..., None], 128, axis=-1).astype(np.float32)
 
 
 def halves(value):
@@ -52,34 +53,59 @@
     return one - two, both - one - two
 
 
-def born_kernel(
+def step_kernel(
     axis_sizes,
     green,
+    hopping_hbm,
+    onsite_hbm,
+    coupling_hbm,
+    damping_hbm,
+    occupation_hbm,
+    tile_map_hbm,
+    previous_hbm,
+    tables_hbm,
+    out,
+    potential_out,
     hopping,
     onsite,
     coupling,
     damping,
     occupation,
-    out,
+    tile_map,
+    previous,
+    tables,
+    load,
     from_left,
     from_right,
     self_energy,
+    relay,
     facts,
     columns,
     block,
     phonon,
+    stencil,
+    densities,
+    weighted,
+    landed,
     slab_send,
     slab_recv,
     energy_send,
     energy_recv,
+    relay_recv,
+    forward_send,
     fact_send,
     fact_recv,
+    density_send,
+    density_recv,
+    plane_send,
+    plane_recv,
 ):
     energies, slabs = axis_sizes
     e, s = lax.axis_index("energy"), lax.axis_index("slab")
     here = hopping.shape[-1]
     chunks = here // ROWS
     owned = 2
+    half = energies // 2
     has = {
         "left": s > 0,
         "right": s < slabs - 1,
@@ -87,20 +113,43 @@
         "above": e < energies - 1,
     }
     device = {"left": (e, s - 1), "right": (e, s + 1), "below": (e - 1, s), "above": (e + 1, s)}
+    crosses = {"above": e == half - 1, "below": e == half}
+    relays = (e == 0) | (e == energies - 1)
+
+    barrier = pltpu.get_barrier_semaphore()
+    for d in range(1, energies):
+        pl.semaphore_signal(
+            barrier, inc=1, device_id=(lax.rem(e + d, energies), s), device_id_type=MESH
+        )
+    for d in range(1, slabs):
+        pl.semaphore_signal(
+            barrier, inc=1, device_id=(e, lax.rem(s + d, slabs)), device_id_type=MESH
+        )
+
+    def loads():
+        pairs = (
+            (coupling_hbm, coupling),
+            (damping_hbm, damping),
+            (occupation_hbm, occupation),
+            (onsite_hbm, onsite),
+            (previous_hbm, previous),
+            (tile_map_hbm, tile_map),
+            (hopping_hbm, hopping),
+            (tables_hbm.at[s], tables),
+        )
+        return [pltpu.make_async_copy(a, b, load.at[i]) for i, (a, b) in enumerate(pairs)]
+
+    for copy in loads():
+        copy.start()
+    for copy in loads():
+        copy.wait()
 
     facts[3, 0:1, :] = coupling[...]
     for k in range(owned):
-        facts[3, 1 + k : 2 + k, :] = jnp.full((1, here), damping[0, k], F32)
-        facts[3, 3 + k : 4 + k, :] = jnp.full((1, here), occupation[0, k], F32)
-
-    barrier = pltpu.get_barrier_semaphore()
-    for side in ("left", "right", "below", "above"):
-
-        @pl.when(has[side])
-        def _():
-            pl.semaphore_signal(barrier, inc=1, device_id=device[side], device_id_type=MESH)
-
-    pl.semaphore_wait(barrier, sum(has[side].astype(jnp.int32) for side in has))
+        facts[3, 1 + k : 2 + k, :] = jnp.broadcast_to(damping[:, k : k + 1], (1, here))
+        facts[3, 3 + k : 4 + k, :] = jnp.broadcast_to(occupation[:, k : k + 1], (1, here))
+
+    pl.semaphore_wait(barrier, energies + slabs - 2)
 
     def slab_copy(side, c):
         k, row = c // chunks, pl.multiple_of(lax.rem(c, chunks) * ROWS, ROWS)
@@ -127,6 +176,41 @@
             device_id_type=MESH,
         )
 
+    def relay_copy(side, c):
+        k, row = c // chunks, pl.multiple_of(lax.rem(c, chunks) * ROWS, ROWS)
+        index = 0 if side == "above" else 1
+        return pltpu.make_async_remote_copy(
+            src_ref=self_energy.at[0, k, :, pl.ds(row, ROWS), :],
+            dst_ref=relay.at[c // 2],
+            send_sem=energy_send.at[index, c],
+            recv_sem=relay_recv.at[c // 2],
+            device_id=(energies - 1 if side == "above" else 0, s),
+            device_id_type=MESH,
+        )
+
+    def forward_copy(side, c):
+        k, row = c // chunks, pl.multiple_of(lax.rem(c, chunks) * ROWS, ROWS)
+        index = 0 if side == "above" else 1
+        return pltpu.make_async_remote_copy(
+            src_ref=relay.at[c // 2],
+            dst_ref=self_energy.at[1 + index, k, :, pl.ds(row, ROWS), :],
+            send_sem=forward_send.at[c // 2],
+            recv_sem=energy_recv.at[index, c],
+            device_id=(half if side == "above" else half - 1, s),
+            device_id_type=MESH,
+        )
+
+    def forward(c):
+        @pl.when(e == energies - 1)
+        def _():
+            relay_copy("above", c).wait_recv()
+            forward_copy("above", c).start()
+
+        @pl.when(e == 0)
+        def _():
+            relay_copy("below", c).wait_recv()
+            forward_copy("below", c).start()
+
     def fact_copy(side):
         index = {"right": 0, "above": 1, "below": 2}[side]
         return pltpu.make_async_remote_copy(
@@ -160,6 +244,32 @@
         @pl.when(has[side])
         def _():
             fact_copy(side).start()
+
+    tall = potential_out.shape[1]
+    width = potential_out.shape[2]
+
+    def blocks(ref):
+        own = ref[0, pl.ds(pl.multiple_of(e * tall, tall), tall), :]
+        before = ref[0, pl.ds(pl.multiple_of(jnp.maximum(e - 1, 0) * tall, tall), tall), :]
+        after = ref[
+            0, pl.ds(pl.multiple_of(jnp.minimum(e + 1, energies - 1) * tall, tall), tall), :
+        ]
+        return before, own, after
+
+    cell = lax.broadcasted_iota(jnp.int32, (3 * tall, width), 1)
+    line = lax.broadcasted_iota(jnp.int32, (3 * tall, width), 0) + (e - 1) * tall
+    inside = (line >= 0) & (line < energies * tall)
+
+    def beside(field):
+        up = pltpu.roll(field, 1, 0)
+        down = pltpu.roll(field, 3 * tall - 1, 0)
+        left = jnp.where(cell == 0, 0.0, pltpu.roll(field, 1, 1))
+        right = jnp.where(cell == width - 1, 0.0, pltpu.roll(field, width - 1, 1))
+        return up + down + left + right
+
+    potential = jnp.where(inside, jnp.concatenate(blocks(previous), axis=0), 0.0)
+    potential = jnp.where(inside, beside(potential), 0.0)
+    stencil[...] = (ANISO * ANISO) * beside(potential)[tall : 2 * tall]
 
     rows = lax.broadcasted_iota(jnp.int32, (here, here), 0)
     lanes = lax.broadcasted_iota(jnp.int32, (here, here), 1)
@@ -204,9 +314,23 @@
             )
         for side in ("above", "below"):
 
-            @pl.when(has[side])
+            bent = crosses[side] & (lax.rem(c, 2) == 1)
+
+            @pl.when(has[side] & jnp.logical_not(bent))
             def _():
                 energy_copy(side, c).start()
+
+            @pl.when(bent)
+            def _():
+                relay_copy(side, c).start()
+
+        @pl.when((lax.rem(c, 2) == 1) & (c >= 3))
+        def _():
+            forward(c - 2)
+
+        @pl.when(c == owned * chunks - 1)
+        def _():
+            forward(c)
 
         return carry
 
@@ -218,14 +342,15 @@
     def step(t, carry):
         k, kind = t // 3, lax.rem(t, 3)
         lax.fori_loop(
-            jnp.where(t == 0, 0, jnp.minimum(owned * chunks - 3 + t, owned * chunks)),
-            jnp.minimum(owned * chunks - 2 + t, owned * chunks),
+            jnp.where(t == 0, 0, jnp.minimum(10 + 2 * t, owned * chunks)),
+            jnp.minimum(12 + 2 * t, owned * chunks),
             form_self_energy,
             0,
         )
-        slot = jnp.where(kind == 2, 0, 1 + kind)
-        fact = jnp.where(kind == 2, 3, 1 + kind)
-        present = jnp.where(kind == 0, e, jnp.where(kind == 1, energies - 1 - e, 1)) > 0
+        side = jnp.where(lax.rem(e, half) >= half // 2, kind, 1 - kind)
+        slot = jnp.where(kind == 2, 0, 1 + side)
+        fact = jnp.where(kind == 2, 3, 1 + side)
+        present = (kind == 2) | (jnp.where(side == 0, e, energies - 1 - e) > 0)
 
         def arrive(side):
             def one(c, inner):
@@ -238,11 +363,11 @@
             def _():
                 fact_copy(side).wait_recv()
 
-        @pl.when((kind == 0) & has["below"])
+        @pl.when((kind < 2) & (side == 0) & has["below"])
         def _():
             arrive("above")
 
-        @pl.when((kind == 1) & has["above"])
+        @pl.when((kind < 2) & (side == 1) & has["above"])
         def _():
             arrive("below")
 
@@ -252,7 +377,7 @@
 
         @pl.when(present)
         def _():
-            place = owned * (e + jnp.where(kind == 2, 0, 2 * kind - 1)) + k
+            place = owned * (e + jnp.where(kind == 2, 0, 2 * side - 1)) + k
             energy = -2.0 + 4.0 * (place.astype(F32) + 0.5) / (owned * energies)
             damp = facts[fact, pl.ds(1 + k, 1), :]
             x_real, x_imag = diagonal_inverse(energy, onsite[...], damp)
@@ -332,77 +457,11 @@
             def _():
                 energy_copy(side, c).wait_send()
 
+        @pl.when(relays & (lax.rem(c, 2) == 1))
+        def _():
+            forward_copy("above", c).wait_send()
+
         return carry
-
-    lax.fori_loop(0, owned * chunks, settle, 0)
-    for side in ("right", "above", "below"):
-
-        @pl.when(has[side])
-        def _():
-            fact_copy(side).wait_send()
-
-
-def born(axis_sizes, green, hopping, onsite, coupling, damping, occupation):
-    size = hopping.shape[-1]
-    count = 2 * (size // ROWS)
-    vmem, smem = pl.BlockSpec(memory_space=pltpu.VMEM), pl.BlockSpec(memory_space=pltpu.SMEM)
-    return pl.pallas_call(
-        functools.partial(born_kernel, axis_sizes),
-        out_shape=jax.ShapeDtypeStruct((2, size), F32),
-        in_specs=[pl.BlockSpec(memory_space=pl.ANY), vmem, vmem, vmem, smem, smem],
-        out_specs=vmem,
-        scratch_shapes=[
-            pltpu.VMEM((count, 2, ROWS, size), F32),
-            pltpu.VMEM((count, 2, ROWS, size), F32),
-            pltpu.VMEM((3, 2, 2, size, size), F32),
-            pltpu.VMEM((4, 8, size), F32),
-            pltpu.VMEM((size, 128), F32),
-            pltpu.VMEM((2, size, size), F32),
-            pltpu.VMEM((4, size, size), F32),
-            pltpu.SemaphoreType.DMA((2, count)),
-            pltpu.SemaphoreType.DMA((2, count)),
-            pltpu.SemaphoreType.DMA((2, count)),
-            pltpu.SemaphoreType.DMA((2, count)),
-            pltpu.SemaphoreType.DMA((3,)),
-            pltpu.SemaphoreType.DMA((3,)),
-        ],
-        compiler_params=pltpu.CompilerParams(
-            collective_id=0, has_side_effects=True, vmem_limit_bytes=50 << 20
-        ),
-        name="born",
-    )(green, hopping, onsite, coupling, damping, occupation)
-
-
-def poisson_kernel(
-    axis_sizes,
-    lesser,
-    tile_map,
-    previous,
-    tables,
-    out,
-    densities,
-    weighted,
-    landed,
-    density_send,
-    density_recv,
-    plane_send,
-    plane_recv,
-):
-    energies, slabs = axis_sizes
-    e, s = lax.axis_index("energy"), lax.axis_index("slab")
-    rows = out.shape[1]
-    width = out.shape[2]
-    barrier = pltpu.get_barrier_semaphore()
-    for d in range(1, energies):
-        pl.semaphore_signal(
-            barrier, inc=1, device_id=(lax.rem(e + d, energies), s), device_id_type=MESH
-        )
-    for d in range(1, slabs):
-        pl.semaphore_signal(
-            barrier, inc=1, device_id=(e, lax.rem(s + d, slabs)), device_id_type=MESH
-        )
-    densities[e] = (4.0 / (2 * energies)) * jnp.sum(lesser[...], axis=0, keepdims=True)
-    pl.semaphore_wait(barrier, energies + slabs - 2)
 
     def density_copy(d):
         return pltpu.make_async_remote_copy(
@@ -435,81 +494,92 @@
             device_id_type=MESH,
         )
 
+    densities[e] = (4.0 / (owned * energies)) * jnp.sum(out[...], axis=0, keepdims=True)
     for d in range(1, energies):
         density_copy(d).start()
-
-    def blocks(ref):
-        own = ref[0, pl.ds(pl.multiple_of(e * rows, rows), rows), :]
-        before = ref[0, pl.ds(pl.multiple_of(jnp.maximum(e - 1, 0) * rows, rows), rows), :]
-        after = ref[
-            0, pl.ds(pl.multiple_of(jnp.minimum(e + 1, energies - 1) * rows, rows), rows), :
-        ]
-        return before, own, after
-
-    lane = lax.broadcasted_iota(jnp.int32, (3 * rows, width), 1)
-    line = lax.broadcasted_iota(jnp.int32, (3 * rows, width), 0) + (e - 1) * rows
-    inside = (line >= 0) & (line < energies * rows)
-
-    def beside(field):
-        up = pltpu.roll(field, 1, 0)
-        down = pltpu.roll(field, 3 * rows - 1, 0)
-        left = jnp.where(lane == 0, 0.0, pltpu.roll(field, 1, 1))
-        right = jnp.where(lane == width - 1, 0.0, pltpu.roll(field, width - 1, 1))
-        return up + down + left + right
-
-    potential = jnp.where(inside, jnp.concatenate(blocks(previous), axis=0), 0.0)
-    potential = jnp.where(inside, beside(potential), 0.0)
-    potential = (ANISO * ANISO) * beside(potential)[rows : 2 * rows]
-    index = jnp.concatenate(blocks(tile_map), axis=0)
-
     for d in range(1, energies):
         density_landing(d).wait_recv()
     density = CHARGE * jnp.sum(densities[...], axis=0)
 
-    def spread(half):
-        table = jnp.broadcast_to(density[:, half * width : (half + 1) * width], (3 * rows, width))
+    index = jnp.concatenate(blocks(tile_map), axis=0)
+
+    def spread(part):
+        table = jnp.broadcast_to(density[:, part * width : (part + 1) * width], (3 * tall, width))
         return jnp.take_along_axis(table, index & (width - 1), axis=1)
 
     source = jnp.where(inside, jnp.where(index < width, spread(0), spread(1)), 0.0)
-    second = ANISO * beside(source)[rows : 2 * rows] + potential
-    source = source[rows : 2 * rows]
+    second = ANISO * beside(source)[tall : 2 * tall] + stencil[...]
+    source = source[tall : 2 * tall]
     for d in range(1, slabs):
-        weighted[d] = tables[0, s, d] * source + tables[1, s, d] * second
+        weighted[d] = tables[d, 0:1, :] * source + tables[d, 1:2, :] * second
         plane_copy(d).start()
-    total = tables[0, s, 0] * source + tables[1, s, 0] * second
+    total = tables[0, 0:1, :] * source + tables[0, 1:2, :] * second
     for d in range(1, slabs):
         plane_copy(d).wait_recv()
         total = total + landed[d]
-    out[0] = total
+    potential_out[0] = total
+    lax.fori_loop(0, owned * chunks, settle, 0)
+    for side in ("right", "above", "below"):
+
+        @pl.when(has[side])
+        def _():
+            fact_copy(side).wait_send()
+
     for d in range(1, energies):
         density_copy(d).wait_send()
     for d in range(1, slabs):
         plane_copy(d).wait_send()
 
 
-def poisson(axis_sizes, lesser, tile_map, previous, tables):
+def advance(axis_sizes, green, hopping, onsite, coupling, damping, occupation, tile_map, previous, tables):
     energies, slabs = axis_sizes
-    rows, width = tile_map.shape[1] // energies, tile_map.shape[2]
-    vmem, smem = pl.BlockSpec(memory_space=pltpu.VMEM), pl.BlockSpec(memory_space=pltpu.SMEM)
+    size = hopping.shape[-1]
+    count = 2 * (size // ROWS)
+    tall, width = tile_map.shape[1] // energies, tile_map.shape[2]
+    dma, vmem = pltpu.SemaphoreType.DMA, pl.BlockSpec(memory_space=pltpu.VMEM)
+    local = (hopping, onsite, coupling, damping, occupation, tile_map, previous)
     return pl.pallas_call(
-        functools.partial(poisson_kernel, axis_sizes),
-        out_shape=jax.ShapeDtypeStruct((1, rows, width), F32),
-        in_specs=[vmem, vmem, vmem, smem],
-        out_specs=vmem,
+        functools.partial(step_kernel, axis_sizes),
+        out_shape=(
+            jax.ShapeDtypeStruct((2, size), F32),
+            jax.ShapeDtypeStruct((1, tall, width), F32),
+        ),
+        in_specs=[pl.BlockSpec(memory_space=pl.ANY)] * 9,
+        out_specs=(vmem, vmem),
         scratch_shapes=[
-            pltpu.VMEM((energies, 1, lesser.shape[1]), F32),
-            pltpu.VMEM((slabs, rows, width), F32),
-            pltpu.VMEM((slabs, rows, width), F32),
-            pltpu.SemaphoreType.DMA((energies,)),
-            pltpu.SemaphoreType.DMA((energies,)),
-            pltpu.SemaphoreType.DMA((slabs,)),
-            pltpu.SemaphoreType.DMA((slabs,)),
+            *(pltpu.VMEM(array.shape, array.dtype) for array in local),
+            pltpu.VMEM(tables.shape[1:], F32),
+            dma((8,)),
+            pltpu.VMEM((count, 2, ROWS, size), F32),
+            pltpu.VMEM((count, 2, ROWS, size), F32),
+            pltpu.VMEM((3, 2, 2, size, size), F32),
+            pltpu.VMEM((count // 2, 2, ROWS, size), F32),
+            pltpu.VMEM((4, 8, size), F32),
+            pltpu.VMEM((size, 128), F32),
+            pltpu.VMEM((2, size, size), F32),
+            pltpu.VMEM((4, size, size), F32),
+            pltpu.VMEM((tall, width), F32),
+            pltpu.VMEM((energies, 1, size), F32),
+            pltpu.VMEM((slabs, tall, width), F32),
+            pltpu.VMEM((slabs, tall, width), F32),
+            dma((2, count)),
+            dma((2, count)),
+            dma((2, count)),
+            dma((2, count)),
+            dma((count // 2,)),
+            dma((count // 2,)),
+            dma((3,)),
+            dma((3,)),
+            dma((energies,)),
+            dma((energies,)),
+            dma((slabs,)),
+            dma((slabs,)),
         ],
         compiler_params=pltpu.CompilerParams(
-            collective_id=1, has_side_effects=True, vmem_limit_bytes=16 << 20
+            collective_id=0, has_side_effects=True, vmem_limit_bytes=60 << 20
         ),
-        name="poisson",
-    )(lesser, tile_map, previous, tables)
+        name="step",
+    )(green, hopping, onsite, coupling, damping, occupation, tile_map, previous, tables)
 
 
 def solution(mesh):
@@ -517,9 +587,33 @@
     tables = line_tables(axis_sizes[1])
 
     def per_device(onsite, hopping, coupling, green, damping, occupation, tile_map, previous):
-        lesser = born(axis_sizes, green, hopping, onsite, coupling, damping, occupation)
-        potential = poisson(axis_sizes, lesser, tile_map, previous, jnp.asarray(tables))
-        return lesser[None], potential
+        lesser, potential = advance(
+            axis_sizes,
+            green,
+            hopping,
+            onsite,
+            coupling,
+            damping,
+            occupation,
+            tile_map,
+            previous,
+            jnp.asarray(tables),
+        )
+
+        def finish(a, b, c, d):
+            c[0] = a[...]
+            d[...] = b[...]
+
+        return tuple(
+            pl.pallas_call(
+                finish,
+                out_shape=(
+                    jax.ShapeDtypeStruct((1, *lesser.shape), F32),
+                    jax.ShapeDtypeStruct(potential.shape, F32),
+                ),
+                name="finish",
+            )(lesser, potential)
+        )
 
     in_specs = (
         P("slab", None),

time: 90.7 us -> 74.9 us (0.83)
  Pallas kernels: 83.8 us -> 74.2 us
  local copies, waits for them, and re-layouts: 6.02 us -> 0 us
    pallas_call x2, Pallas kernels: 83.8 us -> 74.2 us  [the longest x1 72.9 us: advance(): pl.pallas_call(functools.partial(step_kernel, axis_sizes), out_shape=(jax...]
    unnamed x20 -> x0, local copies, waits for them, and re-layouts: 6.02 us -> none
where the time goes in v1:
time: 74.9 us; the launch traced here: 74.8 us
  Pallas kernels  74.2 us (99%)
    pallas_call x1, Pallas kernels, advance(): pl.pallas_call(functools.partial(step_kernel, axis_sizes), out_shape=(jax...  72.9 us

profile of v1, /device:TPU:1, one launch (start us, length us, event | category | flops | bytes accessed | tf_op | source)
XLA Modules:
  0.0 74.8 jit_solution(8132210078849405925)
XLA Ops:
  0.6 72.9 %step.1 = (f32[2,256]{1,0:T(2,128)}, f32[1,8,128]{2,1,0:T(8,128)}) custom-call(f32[2,1,2,256,256]{4,3,2,1,0:T(8,128)} %green.1, f32[1,256,256]{2,1,0:T(8,128)} %hopping_hbm.1, f32[1,256]{1,0:T(1,128)} %onsite_hbm.1, f32[1,256]{1,0:T(1,128)} %coupling_hbm.1, f32[1,2]{1,0:T(1,128)} %damping_hbm.1, f32[1,2]{1,0:T(1,128)} %occupation_hbm.1, ...), custom_call_target="tpu_custom_call" | custom-call | tf_op jit(solution)/shard_map/step/pallas_call | solution.py:541
  73.5 1.3 %finish.1 = (f32[1,2,256]{2,1,0:T(2,128)}, f32[1,8,128]{2,1,0:T(8,128)}) custom-call(f32[2,256]{1,0:T(2,128)} %get-tuple-element.4.a, f32[1,8,128]{2,1,0:T(8,128)} %get-tuple-element.5.b), custom_call_target="tpu_custom_call" | custom-call | tf_op jit(solution)/shard_map/finish/pallas_call | solution.py:608

commit v2 on v1

--- a/solution.py
+++ b/solution.py
@@ -15,6 +15,7 @@
 CHARGE = 2.0
 ANISO = 0.05
 SCREEN = 0.05
+LAG = 3
 ROWS = 32
 
 
@@ -114,7 +115,13 @@
     }
     device = {"left": (e, s - 1), "right": (e, s + 1), "below": (e - 1, s), "above": (e + 1, s)}
     crosses = {"above": e == half - 1, "below": e == half}
-    relays = (e == 0) | (e == energies - 1)
+
+    def route(c):
+        return jnp.where(lax.rem(c, 4) == 3, 2, lax.rem(c, 2))
+
+    def relays(side, c):
+        return (route(c) > 0) & (e == (energies - route(c) if side == "above" else route(c) - 1))
+
 
     barrier = pltpu.get_barrier_semaphore()
     for d in range(1, energies):
@@ -181,10 +188,10 @@
         index = 0 if side == "above" else 1
         return pltpu.make_async_remote_copy(
             src_ref=self_energy.at[0, k, :, pl.ds(row, ROWS), :],
-            dst_ref=relay.at[c // 2],
+            dst_ref=relay.at[c],
             send_sem=energy_send.at[index, c],
-            recv_sem=relay_recv.at[c // 2],
-            device_id=(energies - 1 if side == "above" else 0, s),
+            recv_sem=relay_recv.at[c],
+            device_id=(energies - route(c) if side == "above" else route(c) - 1, s),
             device_id_type=MESH,
         )
 
@@ -192,24 +199,21 @@
         k, row = c // chunks, pl.multiple_of(lax.rem(c, chunks) * ROWS, ROWS)
         index = 0 if side == "above" else 1
         return pltpu.make_async_remote_copy(
-            src_ref=relay.at[c // 2],
+            src_ref=relay.at[c],
             dst_ref=self_energy.at[1 + index, k, :, pl.ds(row, ROWS), :],
-            send_sem=forward_send.at[c // 2],
+            send_sem=forward_send.at[c],
             recv_sem=energy_recv.at[index, c],
             device_id=(half if side == "above" else half - 1, s),
             device_id_type=MESH,
         )
 
     def forward(c):
-        @pl.when(e == energies - 1)
-        def _():
-            relay_copy("above", c).wait_recv()
-            forward_copy("above", c).start()
-
-        @pl.when(e == 0)
-        def _():
-            relay_copy("below", c).wait_recv()
-            forward_copy("below", c).start()
+        for side in ("above", "below"):
+
+            @pl.when(relays(side, c))
+            def _():
+                relay_copy(side, c).wait_recv()
+                forward_copy(side, c).start()
 
     def fact_copy(side):
         index = {"right": 0, "above": 1, "below": 2}[side]
@@ -314,7 +318,7 @@
             )
         for side in ("above", "below"):
 
-            bent = crosses[side] & (lax.rem(c, 2) == 1)
+            bent = crosses[side] & (route(c) > 0)
 
             @pl.when(has[side] & jnp.logical_not(bent))
             def _():
@@ -324,13 +328,9 @@
             def _():
                 relay_copy(side, c).start()
 
-        @pl.when((lax.rem(c, 2) == 1) & (c >= 3))
-        def _():
-            forward(c - 2)
-
-        @pl.when(c == owned * chunks - 1)
-        def _():
-            forward(c)
+        @pl.when(c >= LAG)
+        def _():
+            forward(c - LAG)
 
         return carry
 
@@ -342,11 +342,17 @@
     def step(t, carry):
         k, kind = t // 3, lax.rem(t, 3)
         lax.fori_loop(
-            jnp.where(t == 0, 0, jnp.minimum(10 + 2 * t, owned * chunks)),
-            jnp.minimum(12 + 2 * t, owned * chunks),
+            jnp.where(t == 0, 0, jnp.minimum(12 + 2 * t, owned * chunks)),
+            jnp.minimum(14 + 2 * t, owned * chunks),
             form_self_energy,
             0,
         )
+
+        @pl.when(t == 1)
+        def _():
+            for c in range(owned * chunks - LAG, owned * chunks):
+                forward(c)
+
         side = jnp.where(lax.rem(e, half) >= half // 2, kind, 1 - kind)
         slot = jnp.where(kind == 2, 0, 1 + side)
         fact = jnp.where(kind == 2, 3, 1 + side)
@@ -457,7 +463,7 @@
             def _():
                 energy_copy(side, c).wait_send()
 
-        @pl.when(relays & (lax.rem(c, 2) == 1))
+        @pl.when(relays("above", c) | relays("below", c))
         def _():
             forward_copy("above", c).wait_send()
 
@@ -553,7 +559,7 @@
             pltpu.VMEM((count, 2, ROWS, size), F32),
             pltpu.VMEM((count, 2, ROWS, size), F32),
             pltpu.VMEM((3, 2, 2, size, size), F32),
-            pltpu.VMEM((count // 2, 2, ROWS, size), F32),
+            pltpu.VMEM((count, 2, ROWS, size), F32),
             pltpu.VMEM((4, 8, size), F32),
             pltpu.VMEM((size, 128), F32),
             pltpu.VMEM((2, size, size), F32),
@@ -566,8 +572,8 @@
             dma((2, count)),
             dma((2, count)),
             dma((2, count)),
-            dma((count // 2,)),
-            dma((count // 2,)),
+            dma((count,)),
+            dma((count,)),
             dma((3,)),
             dma((3,)),
             dma((energies,)),

time: 74.9 us -> 72.8 us (0.972)
  Pallas kernels: 74.2 us -> 72 us
    pallas_call x1, Pallas kernels: 72.9 us -> 70.7 us  [advance(): pl.pallas_call(functools.partial(step_kernel, axis_sizes), out_shape=(jax...]
where the time goes in v2:
time: 72.8 us; the launch traced here: 72.6 us
  Pallas kernels  72 us (99%)
    pallas_call x1, Pallas kernels, advance(): pl.pallas_call(functools.partial(step_kernel, axis_sizes), out_shape=(jax...  70.7 us

profile of v2, /device:TPU:1, one launch (start us, length us, event | category | flops | bytes accessed | tf_op | source)
XLA Modules:
  0.0 72.6 jit_solution(2343366356436044716)
XLA Ops:
  0.6 70.7 %step.1 = (f32[2,256]{1,0:T(2,128)}, f32[1,8,128]{2,1,0:T(8,128)}) custom-call(f32[2,1,2,256,256]{4,3,2,1,0:T(8,128)} %green.1, f32[1,256,256]{2,1,0:T(8,128)} %hopping_hbm.1, f32[1,256]{1,0:T(1,128)} %onsite_hbm.1, f32[1,256]{1,0:T(1,128)} %coupling_hbm.1, f32[1,2]{1,0:T(1,128)} %damping_hbm.1, f32[1,2]{1,0:T(1,128)} %occupation_hbm.1, ...), custom_call_target="tpu_custom_call" | custom-call | tf_op jit(solution)/shard_map/step/pallas_call | solution.py:547
  71.3 1.3 %finish.1 = (f32[1,2,256]{2,1,0:T(2,128)}, f32[1,8,128]{2,1,0:T(8,128)}) custom-call(f32[2,256]{1,0:T(2,128)} %get-tuple-element.4.a, f32[1,8,128]{2,1,0:T(8,128)} %get-tuple-element.5.b), custom_call_target="tpu_custom_call" | custom-call | tf_op jit(solution)/shard_map/finish/pallas_call | solution.py:614

commit v3 on v2

--- a/solution.py
+++ b/solution.py
@@ -16,6 +16,7 @@
 ANISO = 0.05
 SCREEN = 0.05
 LAG = 3
+WINDOW = 5
 ROWS = 32
 
 
@@ -27,6 +28,14 @@
     rows = np.arange(count)[:, None]
     weights = np.stack([inverse[rows, around], (inverse @ inverse)[rows, around]], axis=-1)
     return np.repeat(weights[..., None], 128, axis=-1).astype(np.float32)
+
+
+def far_first(count):
+    return sorted(range(1, count), key=lambda d: -min(d % (count // 2), -d % (count // 2)))
+
+
+def middle_first(count):
+    return sorted(range(1, count), key=lambda d: abs(d - count // 2))
 
 
 def halves(value):
@@ -124,11 +133,11 @@
 
 
     barrier = pltpu.get_barrier_semaphore()
-    for d in range(1, energies):
+    for d in far_first(energies):
         pl.semaphore_signal(
             barrier, inc=1, device_id=(lax.rem(e + d, energies), s), device_id_type=MESH
         )
-    for d in range(1, slabs):
+    for d in middle_first(slabs):
         pl.semaphore_signal(
             barrier, inc=1, device_id=(e, lax.rem(s + d, slabs)), device_id_type=MESH
         )
@@ -241,7 +250,7 @@
 
         return carry
 
-    lax.fori_loop(0, owned * chunks, send_green, 0)
+    lax.fori_loop(0, WINDOW, send_green, 0)
 
     for side in ("above", "below"):
 
@@ -310,6 +319,10 @@
         def _():
             slab_copy("left", c).wait_recv()
 
+        @pl.when(c + WINDOW < owned * chunks)
+        def _():
+            send_green(c + WINDOW, 0)
+
         weight_left = columns[pl.ds(row, ROWS), 2:3] * facts[0, 0:1, :]
         weight_right = columns[pl.ds(row, ROWS), 1:2] * facts[3, 0:1, :]
         for part in range(2):
@@ -348,10 +361,11 @@
             0,
         )
 
-        @pl.when(t == 1)
-        def _():
-            for c in range(owned * chunks - LAG, owned * chunks):
-                forward(c)
+        @pl.when(t == 2)
+        def _():
+            forward(owned * chunks - 3)
+            forward(owned * chunks - 2)
+            forward(owned * chunks - 1)
 
         side = jnp.where(lax.rem(e, half) >= half // 2, kind, 1 - kind)
         slot = jnp.where(kind == 2, 0, 1 + side)
@@ -501,7 +515,7 @@
         )
 
     densities[e] = (4.0 / (owned * energies)) * jnp.sum(out[...], axis=0, keepdims=True)
-    for d in range(1, energies):
+    for d in far_first(energies):
         density_copy(d).start()
     for d in range(1, energies):
         density_landing(d).wait_recv()
@@ -516,7 +530,7 @@
     source = jnp.where(inside, jnp.where(index < width, spread(0), spread(1)), 0.0)
     second = ANISO * beside(source)[tall : 2 * tall] + stencil[...]
     source = source[tall : 2 * tall]
-    for d in range(1, slabs):
+    for d in middle_first(slabs):
         weighted[d] = tables[d, 0:1, :] * source + tables[d, 1:2, :] * second
         plane_copy(d).start()
     total = tables[0, 0:1, :] * source + tables[0, 1:2, :] * second

time: 72.8 us -> 71.4 us (0.981)
  Pallas kernels: 72 us -> 70.6 us
    pallas_call x1, Pallas kernels: 70.7 us -> 69.3 us  [advance(): pl.pallas_call(functools.partial(step_kernel, axis_sizes), out_shape=(jax...]
where the time goes in v3:
time: 71.4 us; the launch traced here: 71.2 us
  Pallas kernels  70.6 us (99%)
    pallas_call x1, Pallas kernels, advance(): pl.pallas_call(functools.partial(step_kernel, axis_sizes), out_shape=(jax...  69.3 us

profile of v3, /device:TPU:1, one launch (start us, length us, event | category | flops | bytes accessed | tf_op | source)
XLA Modules:
  0.0 71.2 jit_solution(7456347458902947087)
XLA Ops:
  0.6 69.3 %step.1 = (f32[2,256]{1,0:T(2,128)}, f32[1,8,128]{2,1,0:T(8,128)}) custom-call(f32[2,1,2,256,256]{4,3,2,1,0:T(8,128)} %green.1, f32[1,256,256]{2,1,0:T(8,128)} %hopping_hbm.1, f32[1,256]{1,0:T(1,128)} %onsite_hbm.1, f32[1,256]{1,0:T(1,128)} %coupling_hbm.1, f32[1,2]{1,0:T(1,128)} %damping_hbm.1, f32[1,2]{1,0:T(1,128)} %occupation_hbm.1, ...), custom_call_target="tpu_custom_call" | custom-call | tf_op jit(solution)/shard_map/step/pallas_call | solution.py:561
  70.0 1.3 %finish.1 = (f32[1,2,256]{2,1,0:T(2,128)}, f32[1,8,128]{2,1,0:T(8,128)}) custom-call(f32[2,256]{1,0:T(2,128)} %get-tuple-element.4.a, f32[1,8,128]{2,1,0:T(8,128)} %get-tuple-element.5.b), custom_call_target="tpu_custom_call" | custom-call | tf_op jit(solution)/shard_map/finish/pallas_call | solution.py:628

commit v4 on v3

--- a/solution.py
+++ b/solution.py
@@ -126,7 +126,7 @@
     crosses = {"above": e == half - 1, "below": e == half}
 
     def route(c):
-        return jnp.where(lax.rem(c, 4) == 3, 2, lax.rem(c, 2))
+        return lax.rem(c, 3)
 
     def relays(side, c):
         return (route(c) > 0) & (e == (energies - route(c) if side == "above" else route(c) - 1))

time: 71.4 us -> 70.3 us (0.985)
  Pallas kernels: 70.6 us -> 69.5 us
    pallas_call x1, Pallas kernels: 69.3 us -> 68.2 us  [advance(): pl.pallas_call(functools.partial(step_kernel, axis_sizes), out_shape=(jax...]
where the time goes in v4:
time: 70.3 us; the launch traced here: 70.1 us
  Pallas kernels  69.5 us (99%)
    pallas_call x1, Pallas kernels, advance(): pl.pallas_call(functools.partial(step_kernel, axis_sizes), out_shape=(jax...  68.2 us

profile of v4, /device:TPU:1, one launch (start us, length us, event | category | flops | bytes accessed | tf_op | source)
XLA Modules:
  0.0 70.1 jit_solution(4925233817070555322)
XLA Ops:
  0.6 68.2 %step.1 = (f32[2,256]{1,0:T(2,128)}, f32[1,8,128]{2,1,0:T(8,128)}) custom-call(f32[2,1,2,256,256]{4,3,2,1,0:T(8,128)} %green.1, f32[1,256,256]{2,1,0:T(8,128)} %hopping_hbm.1, f32[1,256]{1,0:T(1,128)} %onsite_hbm.1, f32[1,256]{1,0:T(1,128)} %coupling_hbm.1, f32[1,2]{1,0:T(1,128)} %damping_hbm.1, f32[1,2]{1,0:T(1,128)} %occupation_hbm.1, ...), custom_call_target="tpu_custom_call" | custom-call | tf_op jit(solution)/shard_map/step/pallas_call | solution.py:561
  68.9 1.3 %finish.1 = (f32[1,2,256]{2,1,0:T(2,128)}, f32[1,8,128]{2,1,0:T(8,128)}) custom-call(f32[2,256]{1,0:T(2,128)} %get-tuple-element.4.a, f32[1,8,128]{2,1,0:T(8,128)} %get-tuple-element.5.b), custom_call_target="tpu_custom_call" | custom-call | tf_op jit(solution)/shard_map/finish/pallas_call | solution.py:628

commit v5 on v4

--- a/solution.py
+++ b/solution.py
@@ -126,7 +126,7 @@
     crosses = {"above": e == half - 1, "below": e == half}
 
     def route(c):
-        return lax.rem(c, 3)
+        return lax.rem(owned * chunks - 1 - c, 3)
 
     def relays(side, c):
         return (route(c) > 0) & (e == (energies - route(c) if side == "above" else route(c) - 1))

time: 70.3 us -> 70.7 us (level)
  no operation moved by 1% of the time
where the time goes in v5:
time: 70.7 us; the launch traced here: 70.5 us
  Pallas kernels  69.9 us (99%)
    pallas_call x1, Pallas kernels, advance(): pl.pallas_call(functools.partial(step_kernel, axis_sizes), out_shape=(jax...  68.6 us

profile of v5, /device:TPU:1, one launch (start us, length us, event | category | flops | bytes accessed | tf_op | source)
XLA Modules:
  0.0 70.5 jit_solution(10736737183373284382)
XLA Ops:
  0.6 68.6 %step.1 = (f32[2,256]{1,0:T(2,128)}, f32[1,8,128]{2,1,0:T(8,128)}) custom-call(f32[2,1,2,256,256]{4,3,2,1,0:T(8,128)} %green.1, f32[1,256,256]{2,1,0:T(8,128)} %hopping_hbm.1, f32[1,256]{1,0:T(1,128)} %onsite_hbm.1, f32[1,256]{1,0:T(1,128)} %coupling_hbm.1, f32[1,2]{1,0:T(1,128)} %damping_hbm.1, f32[1,2]{1,0:T(1,128)} %occupation_hbm.1, ...), custom_call_target="tpu_custom_call" | custom-call | tf_op jit(solution)/shard_map/step/pallas_call | solution.py:561
  69.3 1.3 %finish.1 = (f32[1,2,256]{2,1,0:T(2,128)}, f32[1,8,128]{2,1,0:T(8,128)}) custom-call(f32[2,256]{1,0:T(2,128)} %get-tuple-element.4.a, f32[1,8,128]{2,1,0:T(8,128)} %get-tuple-element.5.b), custom_call_target="tpu_custom_call" | custom-call | tf_op jit(solution)/shard_map/finish/pallas_call | solution.py:628
